TPU v7x, 32 devices: a whole 2x2x4 slice. The times are simulated.
32 devices in a mesh: region: 2 (over x), shard: 16 (over z, y, core).
Axes of the slice: x: 2, y: 2, z: 4, core: 2. Of those that a mesh axis runs over, the one named last changes fastest.
Arguments:
- queries: bfloat16 [48, 1024], replicated, may hold values from -6 to 6
- database: bfloat16 [16384, 1024], P(('region', 'shard')), may hold values from -6 to 6
- neighbour_ids: int32 [48, 10], replicated, may hold values from 0 to 16383
- tile_weights: bfloat16 [64, 13, 4, 256], P(('region', 'shard')), may hold values from 0.0019989014 to 0.059814453
- tile_columns: int32 [64, 13, 4, 256], P(('region', 'shard')), may hold values from 0 to 255
- tile_owner: int32 [64, 13], P(('region', 'shard')), may hold values from 0 to 15, all different within a row; in each aligned block of 2 rows (0 to 1, 2 to 3, ...) at most 2 rows name the same one
- tile_block: int32 [64, 13], P(('region', 'shard')), may hold values from 0 to 1
Outputs:
- diffused: float32 [48, 16384], P(None, ('region', 'shard'))
Inputs may be any that keep to these rules, and one draw needn't show every extreme that they name: `tile_owner`: each row names 13 different owners; among the rows of one device's blocks no owner is named more than 2 times, and that many in some devices.
All inputs are finite; a program needn't handle non-finite values.
Results may differ from a plain program's by a relative error of at most 0.005.
Values may be sent and summed in bfloat16 or wider, within the bound.
A program may use at most 64 MiB of HBM per device.

v0:
```python
import math
import jax
import jax.numpy as jnp
from jax import lax
from jax.sharding import PartitionSpec as P

EPS = 1e-06
BETA = 0.8


def unit_rows(matrix):
    return matrix / jnp.sqrt(jnp.sum(matrix * matrix, axis=1, keepdims=True) + EPS)


def per_device(
    queries, database, neighbour_ids, tile_weights, tile_columns, tile_owner, tile_block
):
    rows_dev = database.shape[0]
    feature_width = database.shape[1]
    unit_query = unit_rows(queries.astype(jnp.float32)).astype(jnp.bfloat16)
    first_row = lax.axis_index(("region", "shard")) * rows_dev
    similar = lax.dot_general(
        unit_query, database, (((1,), (1,)), ((), ())), preferred_element_type=jnp.float32
    )
    positive = jnp.maximum(similar, 0.0)
    weights = (positive * positive * positive / math.sqrt(feature_width)).astype(jnp.bfloat16)
    local_ids = neighbour_ids - first_row
    row_ids = lax.broadcasted_iota(jnp.int32, (1, 1, rows_dev), 2)
    counts = jnp.sum((local_ids[:, :, None] == row_ids).astype(jnp.float32), axis=1)
    chosen = (counts * weights.astype(jnp.float32)).astype(jnp.bfloat16)
    local_term = jnp.dot(chosen, database, preferred_element_type=jnp.float32)
    expanded_sum = lax.psum(local_term, ("region", "shard")) + unit_query.astype(jnp.float32)
    expanded = unit_rows(expanded_sum).astype(jnp.bfloat16)
    products = lax.dot_general(
        expanded, database, (((1,), (1,)), ((), ())), preferred_element_type=jnp.float32
    )
    scores = jnp.maximum(products, 0.0).astype(jnp.bfloat16)
    blocks_dev = tile_columns.shape[0]
    tile_count = tile_columns.shape[1]
    edge_count = tile_columns.shape[2]
    block_rows = tile_columns.shape[3]
    query_count = scores.shape[0]
    score_blocks = scores.reshape(query_count, blocks_dev, block_rows)
    owners = tile_owner.reshape(-1)
    block_ids = tile_block.reshape(-1)
    sources = owners * blocks_dev + block_ids

    def fetch_blocks(current):
        region_blocks = lax.all_gather(current, "shard", axis=1, tiled=True)
        return region_blocks.reshape(query_count, -1)

    column_base = (sources * block_rows).reshape(blocks_dev, tile_count, 1, 1)
    flat_columns = column_base + tile_columns

    def spread(current):
        flat = fetch_blocks(current)
        total = jnp.zeros((query_count, blocks_dev, block_rows), jnp.float32)
        for edge in range(edge_count):
            reached = jnp.take(flat, flat_columns[:, :, edge, :], axis=1)
            scaled = (
                reached.astype(jnp.float32) * tile_weights[:, :, edge, :].astype(jnp.float32)[None]
            )
            total = total + jnp.sum(scaled, axis=2)
        return total

    source = score_blocks.astype(jnp.float32)
    current = score_blocks
    current = (source + BETA * spread(current)).astype(jnp.bfloat16)
    diffused = source + BETA * spread(current)
    return diffused.reshape(query_count, blocks_dev * block_rows)


def solution(mesh):
    placed = (
        P(),
        P(("region", "shard"), None),
        P(),
        P(("region", "shard"), None, None, None),
        P(("region", "shard"), None, None, None),
        P(("region", "shard"), None),
        P(("region", "shard"), None),
    )
    return jax.shard_map(
        per_device,
        mesh=mesh,
        in_specs=placed,
        out_specs=P(None, ("region", "shard")),
        check_vma=False,
    )
```

profile of v0, /device:TPU:0, one launch (start us, length us, event | category | flops | bytes accessed | tf_op | source)
XLA Modules:
  0.0 358.0 jit_solution(2654204438736871811)
XLA Ops:
  6.5 0.0 all-reduce.2.cloned.1.call-start
  6.6 0.8 broadcast_subtract_fusion
  7.4 0.2 convert_reduce_fusion
  7.5 1.0 fusion.1
  8.6 0.0 copy-start.16
  8.6 2.3 fusion.8
  10.9 0.0 all-reduce.2.cloned.1.call-update
  10.9 0.0 copy-done.25
  10.9 0.0 copy-done.24
  11.0 0.1 broadcast_add_fusion
  11.1 0.1 fusion.21
  11.1 0.1 compare_and_fusion
  11.3 0.1 fusion.22
  11.4 0.1 compare_and_fusion.2
  11.5 0.6 pad_clamp_fusion.2
  12.1 0.6 copy.164
  12.7 0.6 pad_clamp_fusion.1
  13.3 0.6 copy.172
  13.9 0.6 copy.179
  14.5 0.6 fusion.14
  15.2 0.6 fusion.12
  15.8 0.6 pad_clamp_fusion
  16.4 123.9 %all-reduce.2.cloned.1.call-done = f32[48,1024]{1,0:T(8,128)} async-done(((f32[48,1024]{1,0:T(8,128)}), f32[48,1024]{1,0:T(8,128)}) %all-reduce.2.cloned.1.call-update) | async-done | bytes 196624 | tf_op jit(solution)/shard_map/psum | solution.py:32
  140.3 1.1 multiply_reduce_fusion.8
  141.4 1.4 fusion
  142.8 25.9 %all_gather.6 = bf16[48,32,256]{2,0,1:T(8,128)(2,1)} all-gather(bf16[48,2,256]{2,0,1:T(8,128)(2,1)S(1)} %bitcast.89), channel_id=1, replica_groups=mesh['region'=2,'shard'=16] {'shard'}, dimensions={1}, use_global_device_ids=true | all-gather | bytes 835584 | tf_op jit(solution)/shard_map/all_gather | solution.py:49
  168.7 2.0 copy.158
  170.7 14.2 %gather_fusion = bf16[6656,48]{1,0:T(8,128)(2,1)} fusion(bf16[48,8192]{0,1:T(8,128)(2,1)S(1)} %bitcast.70, s32[7168]{0:T(1024)S(1)} %pad_clamp_fusion.3), kind=kCustom, calls=%fused_computation.clone | custom fusion | bytes 1304576 | tf_op jit(solution)/shard_map/jit(_take)/gather | solution.py:59
  184.9 0.0 copy-done.14
  184.9 5.3 %multiply_reduce_fusion.7 = f32[48,2,256]{0,2,1:T(8,128)S(1)} fusion(bf16[2,13,256,48]{3,2,1,0:T(8,128)(2,1)} %bitcast.84, f32[2,13,256]{2,1,0:T(8,128)S(1)} %get-tuple-element.29, pred[2,13,256]{2,1,0:T(8,128)(4,1)S(1)} %copy.154), kind=kLoop, calls=%fused_computation.15 | loop fusion | flops 1253376 | bytes 770560 | tf_op jit(solution)/shard_map/reduce_sum | solution.py:63
  190.2 0.1 copy.169
  190.3 15.4 %gather_fusion.1 = bf16[6656,48]{1,0:T(8,128)(2,1)} fusion(bf16[48,8192]{0,1:T(8,128)(2,1)S(1)} %bitcast.71, s32[7168]{0:T(1024)} %pad_clamp_fusion.2), kind=kCustom, calls=%fused_computation.1.clone | custom fusion | bytes 1304576 | tf_op jit(solution)/shard_map/jit(_take)/gather | solution.py:59
  205.7 5.4 %multiply_reduce_fusion.6 = f32[48,2,256]{0,2,1:T(8,128)S(1)} fusion(bf16[2,13,256,48]{3,2,1,0:T(8,128)(2,1)} %bitcast.83, f32[2,13,256]{2,1,0:T(8,128)} %get-tuple-element.28, pred[2,13,256]{2,1,0:T(8,128)(4,1)} %copy.164), kind=kLoop, calls=%fused_computation.14 | loop fusion | flops 1253376 | bytes 770560 | tf_op jit(solution)/shard_map/reduce_sum | solution.py:63
  211.1 0.7 copy.170
  211.8 15.4 %gather_fusion.2 = bf16[6656,48]{1,0:T(8,128)(2,1)} fusion(bf16[48,8192]{0,1:T(8,128)(2,1)S(1)} %bitcast.72, s32[7168]{0:T(1024)} %pad_clamp_fusion.1), kind=kCustom, calls=%fused_computation.2.clone | custom fusion | bytes 1304576 | tf_op jit(solution)/shard_map/jit(_take)/gather | solution.py:59
  227.2 5.4 %multiply_reduce_fusion.5 = f32[48,2,256]{0,2,1:T(8,128)S(1)} fusion(bf16[2,13,256,48]{3,2,1,0:T(8,128)(2,1)} %bitcast.85, f32[2,13,256]{2,1,0:T(8,128)} %get-tuple-element.27, pred[2,13,256]{2,1,0:T(8,128)(4,1)} %copy.172), kind=kLoop, calls=%fused_computation.13 | loop fusion | flops 1253376 | bytes 770560 | tf_op jit(solution)/shard_map/reduce_sum | solution.py:63
  232.6 0.8 copy.177
  233.4 15.5 %gather_fusion.3 = bf16[6656,48]{1,0:T(8,128)(2,1)} fusion(bf16[48,8192]{0,1:T(8,128)(2,1)S(1)} %bitcast.73, s32[7168]{0:T(1024)} %pad_clamp_fusion), kind=kCustom, calls=%fused_computation.3.clone | custom fusion | bytes 1304576 | tf_op jit(solution)/shard_map/jit(_take)/gather | solution.py:59
  248.9 0.0 copy-done.22
  248.9 5.4 %multiply_reduce_fusion.4 = f32[48,2,256]{0,2,1:T(8,128)S(1)} fusion(bf16[2,13,256,48]{3,2,1,0:T(8,128)(2,1)} %bitcast.82, f32[2,13,256]{2,1,0:T(8,128)S(1)} %copy-done.11, pred[2,13,256]{2,1,0:T(8,128)(4,1)S(1)} %copy-done.22), kind=kLoop, calls=%fused_computation.12 | loop fusion | flops 1253376 | bytes 770560 | tf_op jit(solution)/shard_map/reduce_sum | solution.py:63
  254.3 0.1 copy.184
  254.4 0.0 copy-done.4
  254.5 21.0 %all_gather.7 = bf16[48,32,256]{2,0,1:T(8,128)(2,1)} all-gather(bf16[48,2,256]{2,0,1:T(8,128)(2,1)S(1)} %add_convert_fusion), channel_id=1, replica_groups=mesh['region'=2,'shard'=16] {'shard'}, dimensions={1}, use_global_device_ids=true | all-gather | bytes 835584 | tf_op jit(solution)/shard_map/all_gather | solution.py:49
  275.5 2.0 copy.185
  277.4 0.0 copy-done.7
  277.5 0.0 copy-start.8
  277.5 14.2 %gather_fusion.4 = bf16[6656,48]{1,0:T(8,128)(2,1)} fusion(bf16[48,8192]{0,1:T(8,128)(2,1)S(1)} %bitcast.74, s32[7168]{0:T(1024)S(1)} %copy-done.7), kind=kCustom, calls=%fused_computation.4.clone | custom fusion | bytes 1304576 | tf_op jit(solution)/shard_map/jit(_take)/gather | solution.py:59
  291.6 0.0 copy-done.8
  291.6 14.1 %gather_fusion.5 = bf16[6656,48]{1,0:T(8,128)(2,1)} fusion(bf16[48,8192]{0,1:T(8,128)(2,1)S(1)} %bitcast.75, s32[7168]{0:T(1024)S(1)} %copy-done.8), kind=kCustom, calls=%fused_computation.5.clone | custom fusion | bytes 1304576 | tf_op jit(solution)/shard_map/jit(_take)/gather | solution.py:59
  305.8 14.1 %gather_fusion.6 = bf16[6656,48]{1,0:T(8,128)(2,1)} fusion(bf16[48,8192]{0,1:T(8,128)(2,1)S(1)} %bitcast.76, s32[7168]{0:T(1024)S(1)} %copy-done.9), kind=kCustom, calls=%fused_computation.6.clone | custom fusion | bytes 1304576 | tf_op jit(solution)/shard_map/jit(_take)/gather | solution.py:59
  319.9 0.0 copy-done.10
  319.9 14.2 %gather_fusion.7 = bf16[6656,48]{1,0:T(8,128)(2,1)} fusion(bf16[48,8192]{0,1:T(8,128)(2,1)S(1)} %bitcast.77, s32[7168]{0:T(1024)S(1)} %copy-done.10), kind=kCustom, calls=%fused_computation.7.clone | custom fusion | bytes 1304576 | tf_op jit(solution)/shard_map/jit(_take)/gather | solution.py:59
  334.1 5.5 %multiply_reduce_fusion.3 = f32[48,2,256]{0,2,1:T(8,128)S(1)} fusion(bf16[2,13,256,48]{3,2,1,0:T(8,128)(2,1)} %bitcast.81, f32[2,13,256]{2,1,0:T(8,128)S(1)} %copy-done.15, pred[2,13,256]{2,1,0:T(8,128)(4,1)S(1)} %copy-done.19), kind=kLoop, calls=%fused_computation.11 | loop fusion | flops 1253376 | bytes 770560 | tf_op jit(solution)/shard_map/reduce_sum | solution.py:63
  339.6 0.1 copy.189
  339.7 0.0 copy-done.2
  339.7 2.4 multiply_reduce_fusion.2
  342.2 0.1 copy.190
  342.3 0.0 copy-done.12
  342.3 5.4 %multiply_reduce_fusion.1 = f32[48,2,256]{0,2,1:T(8,128)S(1)} fusion(bf16[2,13,256,48]{3,2,1,0:T(8,128)(2,1)} %bitcast.79, f32[2,13,256]{2,1,0:T(8,128)S(1)} %copy-done.12, pred[2,13,256]{2,1,0:T(8,128)(4,1)S(1)} %copy-done.21), kind=kLoop, calls=%fused_computation.9 | loop fusion | flops 1253376 | bytes 770560 | tf_op jit(solution)/shard_map/reduce_sum | solution.py:63
  347.7 0.1 copy.193
  347.9 0.0 copy-done.1
  347.9 2.4 multiply_reduce_fusion
  350.3 0.1 copy.196
  350.5 0.7 convert_add_fusion.1
  (56 shorter events, 0.2 us)
Async XLA Ops:
  6.5 2.0 copy-start
  6.5 4.4 %copy-start.25 = (s32[2,13]{1,0:T(2,128)S(1)}, s32[2,13]{1,0:T(2,128)}, u32[]{:S(2)}) copy-start(s32[2,13]{1,0:T(2,128)} %param.14) | copy-start | bytes 316
  6.5 4.4 %copy-start.24 = (s32[2,13]{1,0:T(2,128)S(1)}, s32[2,13]{1,0:T(2,128)}, u32[]{:S(2)}) copy-start(s32[2,13]{1,0:T(2,128)} %param.15) | copy-start | bytes 316
  6.5 4.4 %copy-start.17 = (s32[2,13,4,256]{3,2,1,0:T(4,128)S(1)}, s32[2,13,4,256]{3,2,1,0:T(4,128)}, u32[]{:S(2)}) copy-start(s32[2,13,4,256]{3,2,1,0:T(4,128)} %param.13) | copy-start | bytes 319492
  6.5 133.7 %all-reduce.2.cloned.1.call-start = ((), (), s32[]{:S(2)}) async-start(), calls=%async_computation | async-start | bytes 393216 | tf_op jit(solution)/shard_map/psum | solution.py:32
  8.6 2.7 copy-start.16
  10.9 129.4 %copy-start.3 = (bf16[48,1024]{1,0:T(8,128)(2,1)S(1)}, bf16[48,1024]{1,0:T(8,128)(2,1)}, u32[]{:S(2)}) copy-start(bf16[48,1024]{1,0:T(8,128)(2,1)} %param.9) | copy-start | bytes 294916
  11.3 159.5 %copy-start.6 = (s32[7168]{0:T(1024)}, s32[7168]{0:T(1024)S(1)}, u32[]{:S(2)}) copy-start(s32[7168]{0:T(1024)S(1)} %pad_clamp_fusion.3) | copy-start | bytes 86020
  11.3 173.6 %copy-start.18 = (pred[2,13,256]{2,1,0:T(8,128)(4,1)}, pred[2,13,256]{2,1,0:T(8,128)(4,1)S(1)}, u32[]{:S(2)}) copy-start(pred[2,13,256]{2,1,0:T(8,128)(4,1)S(1)} %copy.154) | copy-start | bytes 19972
  15.2 169.7 %copy-start.14 = (f32[2,13,256]{2,1,0:T(8,128)}, f32[2,13,256]{2,1,0:T(8,128)S(1)}, u32[]{:S(2)}) copy-start(f32[2,13,256]{2,1,0:T(8,128)S(1)} %get-tuple-element.29) | copy-start | bytes 79876
  233.4 15.5 %copy-start.11 = (f32[2,13,256]{2,1,0:T(8,128)S(1)}, f32[2,13,256]{2,1,0:T(8,128)}, u32[]{:S(2)}) copy-start(f32[2,13,256]{2,1,0:T(8,128)} %get-tuple-element.26) | copy-start | bytes 79876
  233.4 15.5 %copy-start.22 = (pred[2,13,256]{2,1,0:T(8,128)(4,1)S(1)}, pred[2,13,256]{2,1,0:T(8,128)(4,1)}, u32[]{:S(2)}) copy-start(pred[2,13,256]{2,1,0:T(8,128)(4,1)} %copy.179) | copy-start | bytes 19972
  248.9 5.5 %copy-start.4 = (f32[48,2,256]{2,0,1:T(8,128)S(1)}, f32[48,2,256]{2,0,1:T(8,128)}, u32[]{:S(2)}) copy-start(f32[48,2,256]{2,0,1:T(8,128)} %copy.170) | copy-start | bytes 294916
  248.9 5.5 %copy-start.5 = (f32[48,2,256]{2,0,1:T(8,128)S(1)}, f32[48,2,256]{2,0,1:T(8,128)}, u32[]{:S(2)}) copy-start(f32[48,2,256]{2,0,1:T(8,128)} %copy.177) | copy-start | bytes 294916
  254.4 23.0 %copy-start.7 = (s32[7168]{0:T(1024)S(1)}, s32[7168]{0:T(1024)}, u32[]{:S(2)}) copy-start(s32[7168]{0:T(1024)} %copy-done.6) | copy-start | bytes 86020
  277.5 14.2 %copy-start.8 = (s32[7168]{0:T(1024)S(1)}, s32[7168]{0:T(1024)}, u32[]{:S(2)}) copy-start(s32[7168]{0:T(1024)} %pad_clamp_fusion.2) | copy-start | bytes 86020
  291.6 14.1 %copy-start.9 = (s32[7168]{0:T(1024)S(1)}, s32[7168]{0:T(1024)}, u32[]{:S(2)}) copy-start(s32[7168]{0:T(1024)} %pad_clamp_fusion.1) | copy-start | bytes 86020
  305.8 14.2 %copy-start.10 = (s32[7168]{0:T(1024)S(1)}, s32[7168]{0:T(1024)}, u32[]{:S(2)}) copy-start(s32[7168]{0:T(1024)} %pad_clamp_fusion) | copy-start | bytes 86020
  319.9 14.2 %copy-start.15 = (f32[2,13,256]{2,1,0:T(8,128)S(1)}, f32[2,13,256]{2,1,0:T(8,128)}, u32[]{:S(2)}) copy-start(f32[2,13,256]{2,1,0:T(8,128)} %copy-done.14) | copy-start | bytes 79876
  319.9 14.2 %copy-start.19 = (pred[2,13,256]{2,1,0:T(8,128)(4,1)S(1)}, pred[2,13,256]{2,1,0:T(8,128)(4,1)}, u32[]{:S(2)}) copy-start(pred[2,13,256]{2,1,0:T(8,128)(4,1)} %copy-done.18) | copy-start | bytes 19972
  334.1 5.6 %copy-start.2 = (bf16[6656,48]{1,0:T(8,128)(2,1)S(1)}, bf16[6656,48]{1,0:T(8,128)(2,1)}, u32[]{:S(2)}) copy-start(bf16[6656,48]{1,0:T(8,128)(2,1)} %gather_fusion.5) | copy-start | bytes 1916932
  334.1 5.6 %copy-start.13 = (f32[2,13,256]{2,1,0:T(8,128)S(1)}, f32[2,13,256]{2,1,0:T(8,128)}, u32[]{:S(2)}) copy-start(f32[2,13,256]{2,1,0:T(8,128)} %get-tuple-element.28) | copy-start | bytes 79876
  334.1 5.6 %copy-start.20 = (pred[2,13,256]{2,1,0:T(8,128)(4,1)S(1)}, pred[2,13,256]{2,1,0:T(8,128)(4,1)}, u32[]{:S(2)}) copy-start(pred[2,13,256]{2,1,0:T(8,128)(4,1)} %copy.164) | copy-start | bytes 19972
  339.6 2.7 copy-start.12
  339.6 2.7 copy-start.21
  342.1 5.7 %copy-start.1 = (bf16[6656,48]{1,0:T(8,128)(2,1)S(1)}, bf16[6656,48]{1,0:T(8,128)(2,1)}, u32[]{:S(2)}) copy-start(bf16[6656,48]{1,0:T(8,128)(2,1)} %gather_fusion.7) | copy-start | bytes 1916932
  342.2 5.7 %copy-start.23 = (pred[2,13,256]{2,1,0:T(8,128)(4,1)S(1)}, pred[2,13,256]{2,1,0:T(8,128)(4,1)}, u32[]{:S(2)}) copy-start(pred[2,13,256]{2,1,0:T(8,128)(4,1)} %copy.179) | copy-start | bytes 19972
Sparse Core Ops, SparseCore 0:
  12.9 127.3 all-reduce.1
where the time goes:
time: 360 us; the launch traced here: 358 us
  local copies, waits for them, and re-layouts  125 us (35%)
  waiting for transfers between devices  124 us (34%)
  blocking collectives  46.9 us (13%)
  other arithmetic  44.3 us (12%)
  between operations  13.9 us (4%)
  matrix products  3.67 us (1%)
    psum x1, waiting for transfers between devices, per_device(): lax.psum(local_term, ('region', 'shard')) + unit_query.astype(jnp.float32)  124 us
    gather x8, local copies, waits for them, and re-layouts, spread(): reached = jnp.take(flat, flat_columns[:, :, edge, :], axis=1)  117 us
    all_gather x2, blocking collectives, fetch_blocks(): region_blocks = lax.all_gather(current, 'shard', axis=1, tiled=True)  46.9 us
    reduce_sum x8, other arithmetic, spread(): total = total + jnp.sum(scaled, axis=2)  37.2 us
  transfers between devices with their start and end apart: 1, of which 1 were waited for; matrix products, arithmetic and copies ran while one was open for 1% of the time, Pallas kernels for 0%

commit v1 on v0

--- a/solution.py
+++ b/solution.py
@@ -6,6 +6,27 @@
 
 EPS = 1e-06
 BETA = 0.8
+
+
+def in_order(pieces, dim):
+    shape = list(pieces.shape[1:])
+    shape[dim] *= pieces.shape[0]
+    return jnp.moveaxis(pieces, 0, dim).reshape(shape)
+
+
+def doubled(shard, axis):
+    size, index = (lax.axis_size(axis), lax.axis_index(axis))
+    tiles, bit = (shard[None], 1)
+    while bit < size:
+        theirs = lax.ppermute(tiles, axis, [(i, i ^ bit) for i in range(size)])
+        low = index & bit == 0
+        tiles = jnp.concatenate([jnp.where(low, tiles, theirs), jnp.where(low, theirs, tiles)])
+        bit *= 2
+    return tiles
+
+
+def gather_by_bits(x, axis, dim):
+    return in_order(doubled(x, axis), dim)
 
 
 def unit_rows(matrix):
@@ -46,7 +67,7 @@
     sources = owners * blocks_dev + block_ids
 
     def fetch_blocks(current):
-        region_blocks = lax.all_gather(current, "shard", axis=1, tiled=True)
+        region_blocks = gather_by_bits(current, "shard", 1)
         return region_blocks.reshape(query_count, -1)
 
     column_base = (sources * block_rows).reshape(blocks_dev, tile_count, 1, 1)

time: 360 us -> 361 us (level)
  waiting for transfers between devices: 124 us -> 183 us
  blocking collectives: 46.9 us -> 0 us
  other arithmetic: 44.3 us -> 31.9 us
  starting transfers between devices: 0.03 us -> 9.77 us
  local copies, waits for them, and re-layouts: 125 us -> 118 us
    ppermute x0 -> x8, waiting for transfers between devices: none -> 54.2 us  [doubled(): theirs = lax.ppermute(tiles, axis, [(i, i ^ bit) for i in range(size)])]
    all_gather x2 -> x0, blocking collectives: 46.9 us -> none  [fetch_blocks(): region_blocks = lax.all_gather(current, 'shard', axis=1, tiled=True)]
    reduce_sum x8, other arithmetic: 37.2 us -> 25.4 us  [spread(): total = total + jnp.sum(scaled, axis=2)]
    ppermute x0 -> x8, starting transfers between devices: none -> 9.73 us  [doubled(): theirs = lax.ppermute(tiles, axis, [(i, i ^ bit) for i in range(size)])]
    psum x1, waiting for transfers between devices: 124 us -> 129 us  [per_device(): lax.psum(local_term, ('region', 'shard')) + unit_query.astype(jnp.float32)]
    all_gather x2 -> x0, local copies, waits for them, and re-layouts: 3.95 us -> none  [fetch_blocks(): region_blocks = lax.all_gather(current, 'shard', axis=1, tiled=True)]
    transpose x0 -> x2, local copies, waits for them, and re-layouts: none -> 3.95 us  [in_order(): return jnp.moveaxis(pieces, 0, dim).reshape(shape)]
    gather x8, local copies, waits for them, and re-layouts: 117 us -> 113 us  [spread(): reached = jnp.take(flat, flat_columns[:, :, edge, :], axis=1)]
  transfers between devices with their start and end apart: 1 -> 9, of which waited for: 1 -> 9; matrix products, arithmetic and copies ran while one was open for 1% -> 0% of each run, Pallas kernels for 0% -> 0%
where the time goes in v1:
time: 361 us
  waiting for transfers between devices  183 us (51%)
  local copies, waits for them, and re-layouts  118 us (33%)
  other arithmetic  31.9 us (9%)
  between operations  14 us (4%)
  starting transfers between devices  9.77 us (3%)
  matrix products  3.72 us (1%)
    psum x1, waiting for transfers between devices, per_device(): lax.psum(local_term, ('region', 'shard')) + unit_query.astype(jnp.float32)  129 us
    gather x8, local copies, waits for them, and re-layouts, spread(): reached = jnp.take(flat, flat_columns[:, :, edge, :], axis=1)  113 us
    ppermute x8, waiting for transfers between devices, doubled(): theirs = lax.ppermute(tiles, axis, [(i, i ^ bit) for i in range(size)])  54.2 us
    reduce_sum x8, other arithmetic, spread(): total = total + jnp.sum(scaled, axis=2)  25.4 us
    ppermute x8, starting transfers between devices, doubled(): theirs = lax.ppermute(tiles, axis, [(i, i ^ bit) for i in range(size)])  9.73 us
  transfers between devices with their start and end apart: 9, of which 9 were waited for; matrix products, arithmetic and copies ran while one was open for 0% of the time, Pallas kernels for 0%

profile of v1, /device:TPU:0, one launch (start us, length us, event | category | flops | bytes accessed | tf_op | source)
XLA Modules:
  0.0 360.9 jit_solution(17580972214215145559)
XLA Ops:
  6.5 0.0 all-reduce.2.cloned.1.call-start
  6.6 0.8 broadcast_subtract_fusion
  7.4 0.2 convert_reduce_fusion
  7.6 1.0 fusion.2
  8.6 0.0 copy-start.7
  8.6 2.3 fusion.9
  10.9 0.0 all-reduce.2.cloned.1.call-update
  11.0 0.1 broadcast_add_fusion
  11.1 0.1 fusion.22
  11.2 0.1 fusion.23
  11.3 0.1 compare_and_fusion.2
  11.4 0.1 compare_and_fusion
  11.5 128.8 %all-reduce.2.cloned.1.call-done = f32[48,1024]{1,0:T(8,128)} async-done(((f32[48,1024]{1,0:T(8,128)}), f32[48,1024]{1,0:T(8,128)}) %all-reduce.2.cloned.1.call-update) | async-done | bytes 196624 | tf_op jit(solution)/shard_map/psum | solution.py:53
  140.3 1.1 multiply_reduce_fusion.8
  141.5 1.4 fusion
  142.9 0.0 copy-start.9
  142.9 0.1 copy.203
  143.0 0.1 collective-permute-start
  143.2 0.3 copy-done.9
  143.5 0.9 collective-permute-done
  144.4 0.1 copy.162
  144.5 0.1 copy.163
  144.7 1.5 collective-permute-start.1
  146.2 3.4 collective-permute-done.1
  149.6 3.4 collective-permute-start.2
  153.0 4.4 %collective-permute-done.2 = bf16[4,48,2,256]{3,1,2,0:T(8,128)(2,1)S(1)} collective-permute-done((bf16[4,48,2,256]{3,1,2,0:T(8,128)(2,1)S(1)}, bf16[4,48,2,256]{3,1,2,0:T(8,128)(2,1)S(1)}, u32[]{:S(2)}, u32[]{:S(2)}) %collective-permute-start.2) | collective-permute-done | bytes 196640 | tf_op jit(solution)/shard_map/ppermute | solution.py:21
  157.5 1.8 collective-permute-start.3
  159.4 17.2 %collective-permute-done.3 = bf16[8,48,2,256]{3,1,2,0:T(8,128)(2,1)S(1)} collective-permute-done((bf16[8,48,2,256]{3,1,2,0:T(8,128)(2,1)S(1)}, bf16[8,48,2,256]{3,1,2,0:T(8,128)(2,1)S(1)}, u32[]{:S(2)}, u32[]{:S(2)}) %collective-permute-start.3) | collective-permute-done | bytes 393248 | tf_op jit(solution)/shard_map/ppermute | solution.py:21
  176.6 0.1 broadcast_select_fusion.3
  176.7 1.0 maximum_bitcast_fusion
  177.6 2.0 copy.164
  179.6 14.2 %gather_fusion.2 = bf16[6656,48]{1,0:T(8,128)(2,1)} fusion(bf16[48,8192]{0,1:T(8,128)(2,1)S(1)} %bitcast.75, s32[7168]{0:T(1024)S(1)} %pad_clamp_fusion.1), kind=kCustom, calls=%fused_computation.2.clone | custom fusion | bytes 1304576 | tf_op jit(solution)/shard_map/jit(_take)/gather | solution.py:80
  193.8 14.1 %gather_fusion.1 = bf16[6656,48]{1,0:T(8,128)(2,1)} fusion(bf16[48,8192]{0,1:T(8,128)(2,1)S(1)} %bitcast.76, s32[7168]{0:T(1024)S(1)} %pad_clamp_fusion.2), kind=kCustom, calls=%fused_computation.1.clone | custom fusion | bytes 1304576 | tf_op jit(solution)/shard_map/jit(_take)/gather | solution.py:80
  207.9 14.2 %gather_fusion = bf16[6656,48]{1,0:T(8,128)(2,1)} fusion(bf16[48,8192]{0,1:T(8,128)(2,1)S(1)} %bitcast.77, s32[7168]{0:T(1024)S(1)} %pad_clamp_fusion.3), kind=kCustom, calls=%fused_computation.clone | custom fusion | bytes 1304576 | tf_op jit(solution)/shard_map/jit(_take)/gather | solution.py:80
  222.1 14.1 %gather_fusion.3 = bf16[6656,48]{1,0:T(8,128)(2,1)} fusion(bf16[48,8192]{0,1:T(8,128)(2,1)S(1)} %bitcast.78, s32[7168]{0:T(1024)S(1)} %pad_clamp_fusion), kind=kCustom, calls=%fused_computation.3.clone | custom fusion | bytes 1304576 | tf_op jit(solution)/shard_map/jit(_take)/gather | solution.py:80
  236.2 5.5 %multiply_reduce_fusion.5 = f32[48,2,256]{0,2,1:T(8,128)S(1)} fusion(bf16[2,13,256,48]{3,2,1,0:T(8,128)(2,1)} %bitcast.86, f32[2,13,256]{2,1,0:T(8,128)S(1)} %get-tuple-element.43, pred[2,13,256]{2,1,0:T(8,128)(4,1)S(1)} %copy.176), kind=kLoop, calls=%fused_computation.13 | loop fusion | flops 1253376 | bytes 770560 | tf_op jit(solution)/shard_map/reduce_sum | solution.py:84
  241.7 2.4 multiply_reduce_fusion.6
  244.1 2.4 multiply_reduce_fusion.7
  246.6 2.4 multiply_reduce_fusion.4
  249.0 0.1 fusion.1
  249.1 0.1 collective-permute-start.4
  249.1 1.3 collective-permute-done.4
  250.5 0.1 copy.187
  250.6 0.1 copy.188
  250.7 1.5 collective-permute-start.5
  252.3 3.4 collective-permute-done.5
  255.7 0.1 collective-permute-start.6
  255.8 6.1 %collective-permute-done.6 = bf16[4,48,2,256]{3,1,2,0:T(8,128)(2,1)S(1)} collective-permute-done((bf16[4,48,2,256]{3,1,2,0:T(8,128)(2,1)S(1)}, bf16[4,48,2,256]{3,1,2,0:T(8,128)(2,1)S(1)}, u32[]{:S(2)}, u32[]{:S(2)}) %collective-permute-start.6) | collective-permute-done | bytes 196640 | tf_op jit(solution)/shard_map/ppermute | solution.py:21
  261.9 1.2 collective-permute-start.7
  263.2 17.6 %collective-permute-done.7 = bf16[8,48,2,256]{3,1,2,0:T(8,128)(2,1)S(1)} collective-permute-done((bf16[8,48,2,256]{3,1,2,0:T(8,128)(2,1)S(1)}, bf16[8,48,2,256]{3,1,2,0:T(8,128)(2,1)S(1)}, u32[]{:S(2)}, u32[]{:S(2)}) %collective-permute-start.7) | collective-permute-done | bytes 393248 | tf_op jit(solution)/shard_map/ppermute | solution.py:21
  280.8 0.1 broadcast_select_fusion.1
  280.8 1.0 maximum_bitcast_fusion.1
  281.8 2.0 copy.189
  283.8 14.2 %gather_fusion.6 = bf16[6656,48]{1,0:T(8,128)(2,1)} fusion(bf16[48,8192]{0,1:T(8,128)(2,1)S(1)} %bitcast.71, s32[7168]{0:T(1024)S(1)} %pad_clamp_fusion.1), kind=kCustom, calls=%fused_computation.6.clone | custom fusion | bytes 1304576 | tf_op jit(solution)/shard_map/jit(_take)/gather | solution.py:80
  298.0 14.1 %gather_fusion.5 = bf16[6656,48]{1,0:T(8,128)(2,1)} fusion(bf16[48,8192]{0,1:T(8,128)(2,1)S(1)} %bitcast.72, s32[7168]{0:T(1024)S(1)} %pad_clamp_fusion.2), kind=kCustom, calls=%fused_computation.5.clone | custom fusion | bytes 1304576 | tf_op jit(solution)/shard_map/jit(_take)/gather | solution.py:80
  312.1 14.2 %gather_fusion.4 = bf16[6656,48]{1,0:T(8,128)(2,1)} fusion(bf16[48,8192]{0,1:T(8,128)(2,1)S(1)} %bitcast.73, s32[7168]{0:T(1024)S(1)} %pad_clamp_fusion.3), kind=kCustom, calls=%fused_computation.4.clone | custom fusion | bytes 1304576 | tf_op jit(solution)/shard_map/jit(_take)/gather | solution.py:80
  326.2 14.1 %gather_fusion.7 = bf16[6656,48]{1,0:T(8,128)(2,1)} fusion(bf16[48,8192]{0,1:T(8,128)(2,1)S(1)} %bitcast.74, s32[7168]{0:T(1024)S(1)} %pad_clamp_fusion), kind=kCustom, calls=%fused_computation.7.clone | custom fusion | bytes 1304576 | tf_op jit(solution)/shard_map/jit(_take)/gather | solution.py:80
  340.4 5.5 %multiply_reduce_fusion.1 = f32[48,2,256]{0,2,1:T(8,128)S(1)} fusion(bf16[2,13,256,48]{3,2,1,0:T(8,128)(2,1)} %bitcast.82, f32[2,13,256]{2,1,0:T(8,128)S(1)} %get-tuple-element.43, pred[2,13,256]{2,1,0:T(8,128)(4,1)S(1)} %copy.176), kind=kLoop, calls=%fused_computation.9 | loop fusion | flops 1253376 | bytes 770560 | tf_op jit(solution)/shard_map/reduce_sum | solution.py:84
  345.9 2.4 multiply_reduce_fusion.2
  348.3 2.4 multiply_reduce_fusion.3
  350.8 2.4 multiply_reduce_fusion
  353.2 0.1 add_multiply_fusion
  353.2 0.1 copy.202
  353.4 0.7 convert_add_fusion.1
  (58 shorter events, 0.5 us)
Async XLA Ops:
  6.5 2.1 copy-start
  6.5 4.4 %copy-start.13 = (s32[2,13]{1,0:T(2,128)S(1)}, s32[2,13]{1,0:T(2,128)}, u32[]{:S(2)}) copy-start(s32[2,13]{1,0:T(2,128)} %param.14) | copy-start | bytes 316
  6.5 4.4 %copy-start.12 = (s32[2,13]{1,0:T(2,128)S(1)}, s32[2,13]{1,0:T(2,128)}, u32[]{:S(2)}) copy-start(s32[2,13]{1,0:T(2,128)} %param.15) | copy-start | bytes 316
  6.5 4.5 %copy-start.11 = (s32[2,13,4,256]{3,2,1,0:T(4,128)S(1)}, s32[2,13,4,256]{3,2,1,0:T(4,128)}, u32[]{:S(2)}) copy-start(s32[2,13,4,256]{3,2,1,0:T(4,128)} %param.13) | copy-start | bytes 319492
  6.5 4.7 %copy-start.8 = (bf16[2,13,4,256]{3,2,1,0:T(4,128)(2,1)S(1)}, bf16[2,13,4,256]{3,2,1,0:T(4,128)(2,1)}, u32[]{:S(2)}) copy-start(bf16[2,13,4,256]{3,2,1,0:T(4,128)(2,1)} %param.12) | copy-start | bytes 159748
  6.5 133.8 %all-reduce.2.cloned.1.call-start = ((), (), s32[]{:S(2)}) async-start(), calls=%async_computation | async-start | bytes 393216 | tf_op jit(solution)/shard_map/psum | solution.py:53
  8.6 131.7 %copy-start.7 = (bf16[48,1024]{1,0:T(8,128)(2,1)S(1)}, bf16[48,1024]{1,0:T(8,128)(2,1)}, u32[]{:S(2)}) copy-start(bf16[48,1024]{1,0:T(8,128)(2,1)} %param.9) | copy-start | bytes 294916
  142.9 0.6 copy-start.9
  143.0 1.4 collective-permute-start
  144.7 4.9 %collective-permute-start.1 = (bf16[2,48,2,256]{3,1,2,0:T(8,128)(2,1)S(1)}, bf16[2,48,2,256]{3,1,2,0:T(8,128)(2,1)S(1)}, u32[]{:S(2)}, u32[]{:S(2)}) collective-permute-start(bf16[2,48,2,256]{3,1,2,0:T(8,128)(2,1)S(1)} %pad_maximum_fusion.4), channel_id=1, source_target_pairs={{0,2},{1,3},{2,0},{3,1},{4,6},{5,7},{6,4},{7,5},{8,10},{9,11},{10,... | collective-permute-start | bytes 294920 | tf_op jit(solution)/shard_map/ppermute | solution.py:21
  149.6 7.8 %collective-permute-start.2 = (bf16[4,48,2,256]{3,1,2,0:T(8,128)(2,1)S(1)}, bf16[4,48,2,256]{3,1,2,0:T(8,128)(2,1)S(1)}, u32[]{:S(2)}, u32[]{:S(2)}) collective-permute-start(bf16[4,48,2,256]{3,1,2,0:T(8,128)(2,1)S(1)} %pad_maximum_fusion.2), channel_id=1, source_target_pairs={{0,4},{1,5},{2,6},{3,7},{4,0},{5,1},{6,2},{7,3},{8,12},{9,13},{10,... | collective-permute-start | bytes 589832 | tf_op jit(solution)/shard_map/ppermute | solution.py:21
  157.5 19.1 %collective-permute-start.3 = (bf16[8,48,2,256]{3,1,2,0:T(8,128)(2,1)S(1)}, bf16[8,48,2,256]{3,1,2,0:T(8,128)(2,1)S(1)}, u32[]{:S(2)}, u32[]{:S(2)}) collective-permute-start(bf16[8,48,2,256]{3,1,2,0:T(8,128)(2,1)S(1)} %pad_maximum_fusion), channel_id=1, source_target_pairs={{0,8},{1,9},{2,10},{3,11},{4,12},{5,13},{6,14},{7,15},{8,0},{9,1},... | collective-permute-start | bytes 1179656 | tf_op jit(solution)/shard_map/ppermute | solution.py:21
  236.2 5.5 %copy-start.6 = (bf16[6656,48]{1,0:T(8,128)(2,1)S(1)}, bf16[6656,48]{1,0:T(8,128)(2,1)}, u32[]{:S(2)}) copy-start(bf16[6656,48]{1,0:T(8,128)(2,1)} %gather_fusion.1) | copy-start | bytes 1916932
  236.2 7.9 %copy-start.5 = (bf16[6656,48]{1,0:T(8,128)(2,1)S(1)}, bf16[6656,48]{1,0:T(8,128)(2,1)}, u32[]{:S(2)}) copy-start(bf16[6656,48]{1,0:T(8,128)(2,1)} %gather_fusion) | copy-start | bytes 1916932
  241.7 4.9 %copy-start.4 = (bf16[6656,48]{1,0:T(8,128)(2,1)S(1)}, bf16[6656,48]{1,0:T(8,128)(2,1)}, u32[]{:S(2)}) copy-start(bf16[6656,48]{1,0:T(8,128)(2,1)} %gather_fusion.3) | copy-start | bytes 1916932
  249.1 1.4 collective-permute-start.4
  250.7 4.9 %collective-permute-start.5 = (bf16[2,48,2,256]{3,1,2,0:T(8,128)(2,1)S(1)}, bf16[2,48,2,256]{3,1,2,0:T(8,128)(2,1)S(1)}, u32[]{:S(2)}, u32[]{:S(2)}) collective-permute-start(bf16[2,48,2,256]{3,1,2,0:T(8,128)(2,1)S(1)} %pad_maximum_fusion.5), channel_id=1, source_target_pairs={{0,2},{1,3},{2,0},{3,1},{4,6},{5,7},{6,4},{7,5},{8,10},{9,11},{10,... | collective-permute-start | bytes 294920 | tf_op jit(solution)/shard_map/ppermute | solution.py:21
  255.7 6.2 %collective-permute-start.6 = (bf16[4,48,2,256]{3,1,2,0:T(8,128)(2,1)S(1)}, bf16[4,48,2,256]{3,1,2,0:T(8,128)(2,1)S(1)}, u32[]{:S(2)}, u32[]{:S(2)}) collective-permute-start(bf16[4,48,2,256]{3,1,2,0:T(8,128)(2,1)S(1)} %pad_maximum_fusion.3), channel_id=1, source_target_pairs={{0,4},{1,5},{2,6},{3,7},{4,0},{5,1},{6,2},{7,3},{8,12},{9,13},{10,... | collective-permute-start | bytes 589832 | tf_op jit(solution)/shard_map/ppermute | solution.py:21
  261.9 18.8 %collective-permute-start.7 = (bf16[8,48,2,256]{3,1,2,0:T(8,128)(2,1)S(1)}, bf16[8,48,2,256]{3,1,2,0:T(8,128)(2,1)S(1)}, u32[]{:S(2)}, u32[]{:S(2)}) collective-permute-start(bf16[8,48,2,256]{3,1,2,0:T(8,128)(2,1)S(1)} %pad_maximum_fusion.1), channel_id=1, source_target_pairs={{0,8},{1,9},{2,10},{3,11},{4,12},{5,13},{6,14},{7,15},{8,0},{9,1},... | collective-permute-start | bytes 1179656 | tf_op jit(solution)/shard_map/ppermute | solution.py:21
  340.4 5.5 %copy-start.3 = (bf16[6656,48]{1,0:T(8,128)(2,1)S(1)}, bf16[6656,48]{1,0:T(8,128)(2,1)}, u32[]{:S(2)}) copy-start(bf16[6656,48]{1,0:T(8,128)(2,1)} %gather_fusion.5) | copy-start | bytes 1916932
  340.4 7.9 %copy-start.2 = (bf16[6656,48]{1,0:T(8,128)(2,1)S(1)}, bf16[6656,48]{1,0:T(8,128)(2,1)}, u32[]{:S(2)}) copy-start(bf16[6656,48]{1,0:T(8,128)(2,1)} %gather_fusion.4) | copy-start | bytes 1916932
  345.9 4.9 %copy-start.1 = (bf16[6656,48]{1,0:T(8,128)(2,1)S(1)}, bf16[6656,48]{1,0:T(8,128)(2,1)}, u32[]{:S(2)}) copy-start(bf16[6656,48]{1,0:T(8,128)(2,1)} %gather_fusion.7) | copy-start | bytes 1916932
  350.8 2.6 copy-start.10
Sparse Core Ops, SparseCore 0:
  12.9 127.3 all-reduce.1
